TPU v7x, 256 devices: a whole 4x4x8 slice. The times are simulated.
256 devices in a mesh: req: 16 (over y_lo, z), tensor: 16 (over y_hi, x, core).
Axes of the slice: x: 4, y: 4 (y_hi: 2, y_lo: 2; y = y_hi * 2 + y_lo), z: 8, core: 2. Of those that a mesh axis runs over, the one named last changes fastest.
Arguments:
- activations: bfloat16 [8192, 8192], P(('req', 'tensor')), parts along dimension 0, may hold values from -6 to 6
- norm_gain: float32 [8192], replicated, may hold values from 0.1 to 1.9
- query_weight: bfloat16 [8192, 4096], P(None, 'tensor'), may hold values from -0.0625 to 0.0625
- keyvalue_weight: bfloat16 [8192, 2048], P(None, 'tensor'), may hold values from -0.0625 to 0.0625
- output_weight: bfloat16 [4096, 8192], P('tensor'), may hold values from -0.09375 to 0.09375
- page_pool: bfloat16 [2048, 128, 256], P(('req', 'tensor')), parts along dimension 0, may hold values from -320 to 320
- page_table: int32 [288, 8], P('req'), parts along dimension 0, may hold values from 0 to 15
- prefill_offsets: int32 [32], P('req'), parts along dimension 0, may hold values from 0 to 1024, as said below
- decode_lengths: int32 [256], P('req'), parts along dimension 0, may hold values from 1 to 1024, as said below
Outputs:
- block_output: bfloat16 [8192, 8192], P(('req', 'tensor')), parts along dimension 0
There are 16 independent parts, one for each index of `req`. A program takes and returns all parts, laid end to end along the dimension named above; an argument that names none is the same for every part. Nothing has to cross between parts.
Inputs may be any that keep to these rules, and one draw needn't show every extreme that they name: `page_table`: pages may be shared between requests. `decode_lengths`: some decode request has exactly 1024 cached tokens. `prefill_offsets`: some stretch has exactly 1024 cached tokens before it.
All inputs are finite; a program needn't handle non-finite values.
Results may differ from a plain program's by a relative error of at most 0.0095.
The roundings to bfloat16 on the way count: a program that leaves them out, or rounds other values in their place, can miss the bound.
Values may be sent and summed in bfloat16 or wider, within the bound.
A program may use at most 128 MiB of HBM per device.

v0:
```python
import jax
import jax.numpy as jnp
from jax import lax
from jax.sharding import PartitionSpec as P

QH = 32
KVH = 8
HD = 128
C = 248
eps_norm = 1e-06
rope_base = 1000000.0
neg_big = -1e30


def partner(array, axis, distance):
    return lax.ppermute(array, axis, [(i, i ^ 1 << distance) for i in range(lax.axis_size(axis))])


def rotate(values, positions):
    half_dim = values.shape[-1] // 2
    frequency = rope_base ** (-2.0 * jnp.arange(half_dim, dtype=jnp.float32) / values.shape[-1])
    angles = positions.astype(jnp.float32)[:, None] * frequency[None, :]
    cosine = jnp.cos(angles)[:, None, :]
    sine_part = jnp.sin(angles)[:, None, :]
    first_half = values[..., :half_dim]
    second_half = values[..., half_dim:]
    return jnp.concatenate(
        [
            first_half * cosine - second_half * sine_part,
            second_half * cosine + first_half * sine_part,
        ],
        axis=-1,
    )


def cached_block(queries, table_row, key_limit, pool_rows, page_lo):
    held_pages = pool_rows.shape[1]
    page_len = pool_rows.shape[2]
    head_dim = queries.shape[-1]
    local_page = table_row - page_lo
    owned_page = (local_page >= 0) & (local_page < held_pages)
    local_page = jnp.clip(local_page, 0, held_pages - 1)
    fetched = jnp.take(pool_rows, local_page, axis=1)
    key_span = fetched.shape[1] * page_len
    key_rows = fetched.reshape(pool_rows.shape[0], key_span, 2 * head_dim)
    slot_ids = jnp.arange(key_span, dtype=jnp.int32)
    visible = jnp.repeat(owned_page, page_len, total_repeat_length=key_span) & (
        slot_ids < key_limit
    )
    scores = jnp.einsum(
        "rkgd,ksd->kgrs", queries, key_rows[:, :, :head_dim], preferred_element_type=jnp.float32
    ) * head_dim ** (-0.5)
    scores = jnp.where(visible, scores, neg_big)
    highest = jnp.max(scores, axis=-1)
    weights = jnp.where(visible, jnp.exp(scores - highest[..., None]), 0.0)
    totals = jnp.sum(weights, axis=-1)
    blended = jnp.einsum(
        "kgrs,ksd->rkgd",
        weights.astype(jnp.bfloat16),
        key_rows[:, :, head_dim:],
        preferred_element_type=jnp.float32,
    )
    return (jnp.transpose(highest, (2, 0, 1)), jnp.transpose(totals, (2, 0, 1)), blended)


def cached_all(
    queries, pool_rows, page_lo, page_table, prefill_offsets, decode_lengths, stretch_len
):
    pieces = []
    for stretch_id in range(2):
        lower = stretch_id * stretch_len
        pieces.append(
            cached_block(
                queries[lower : lower + stretch_len],
                page_table[stretch_id],
                prefill_offsets[stretch_id],
                pool_rows,
                page_lo,
            )
        )

    def decode_one(decode_item):
        query_row, table_row, length_one = decode_item
        return cached_block(query_row[None], table_row, length_one, pool_rows, page_lo)

    decoded = lax.map(decode_one, (queries[2 * stretch_len :], page_table[2:], decode_lengths))
    decoded = tuple((stacked[:, 0] for stacked in decoded))
    return tuple(
        (
            jnp.concatenate([pieces[0][part_id], pieces[1][part_id], decoded[part_id]], axis=0)
            for part_id in range(3)
        )
    )


def stretch_self(queries, new_keys, new_values):
    length_q = queries.shape[0]
    scores = jnp.einsum(
        "rkgd,skd->kgrs", queries, new_keys, preferred_element_type=jnp.float32
    ) * queries.shape[-1] ** (-0.5)
    counter = jnp.arange(length_q, dtype=jnp.int32)
    causal = counter[:, None] >= counter[None, :]
    scores = jnp.where(causal, scores, neg_big)
    highest = jnp.max(scores, axis=-1)
    weights = jnp.where(causal, jnp.exp(scores - highest[..., None]), 0.0)
    totals = jnp.sum(weights, axis=-1)
    blended = jnp.einsum(
        "kgrs,skd->rkgd",
        weights.astype(jnp.bfloat16),
        new_values,
        preferred_element_type=jnp.float32,
    )
    return (jnp.transpose(highest, (2, 0, 1)), jnp.transpose(totals, (2, 0, 1)), blended)


def fresh_all(queries, new_keys, new_values, stretch_len):
    pieces = []
    for stretch_id in range(2):
        lower = stretch_id * stretch_len
        upper = lower + stretch_len
        pieces.append(
            stretch_self(queries[lower:upper], new_keys[lower:upper], new_values[lower:upper])
        )
    tail_q = queries[2 * stretch_len :]
    own_score = jnp.einsum(
        "rkgd,rkd->rkg", tail_q, new_keys[2 * stretch_len :], preferred_element_type=jnp.float32
    ) * queries.shape[-1] ** (-0.5)
    own_values = jnp.broadcast_to(
        new_values[2 * stretch_len :].astype(jnp.float32)[:, :, None, :], tail_q.shape
    )
    decoded = (own_score, jnp.ones_like(own_score), own_values)
    return tuple(
        (
            jnp.concatenate([pieces[0][part_id], pieces[1][part_id], decoded[part_id]], axis=0)
            for part_id in range(3)
        )
    )


def combine_parts(first, second):
    highest = jnp.maximum(first[0], second[0])
    first_scale = jnp.exp(first[0] - highest)
    second_scale = jnp.exp(second[0] - highest)
    totals = first_scale * first[1] + second_scale * second[1]
    blended = first_scale[..., None] * first[2] + second_scale[..., None] * second[2]
    return (highest, totals, blended)


def shards(
    activations,
    norm_gain,
    query_weight,
    keyvalue_weight,
    output_weight,
    page_pool,
    page_table,
    prefill_offsets,
    decode_lengths,
):
    my_index = lax.axis_index("tensor")
    parity = my_index % 2
    local_q = query_weight.shape[1] // HD
    group = QH // KVH
    widened = activations.astype(jnp.float32)
    normed = (
        widened
        * lax.rsqrt(jnp.mean(widened * widened, axis=-1, keepdims=True) + eps_norm)
        * norm_gain
    ).astype(jnp.bfloat16)
    project_piece = lax.all_gather(normed, "tensor", axis=0, tiled=True)
    joint = jnp.concatenate(
        [
            jnp.dot(project_piece, query_weight, preferred_element_type=jnp.float32),
            jnp.dot(project_piece, keyvalue_weight, preferred_element_type=jnp.float32),
        ],
        axis=1,
    )
    row_count = joint.shape[0]
    inner = jnp.arange(C, dtype=jnp.int32)
    positions = jnp.concatenate(
        [prefill_offsets[0] + inner, prefill_offsets[1] + inner, decode_lengths]
    )
    own_q = rotate(joint[:, : local_q * HD].reshape(row_count, local_q, HD), positions).astype(
        jnp.bfloat16
    )
    kv_cols = joint[:, local_q * HD :]
    kv_local = 1
    turned = rotate(kv_cols[:, None, :], positions)[:, 0, :]
    own_half = jnp.where(parity == 0, turned, kv_cols).astype(jnp.bfloat16)
    other_half = partner(own_half, "tensor", 0)
    new_keys = jnp.where(parity == 0, own_half, other_half)[:, None, :]
    new_values = jnp.where(parity == 0, other_half, own_half)[:, None, :]
    local_pool = page_pool[None]
    own_grouped = own_q.reshape(row_count, kv_local, local_q // kv_local, HD)
    other_q = partner(own_q, "tensor", 0)
    lower_first = jnp.concatenate([own_q, other_q], axis=1)
    upper_first = jnp.concatenate([other_q, own_q], axis=1)
    group_q = jnp.where(parity == 0, lower_first, upper_first).reshape(row_count, 1, group, HD)
    found = cached_all(
        group_q,
        local_pool,
        parity * page_pool.shape[0],
        page_table,
        prefill_offsets,
        decode_lengths,
        C,
    )
    low_part = tuple((piece[:, :, :local_q] for piece in found))
    high_part = tuple((piece[:, :, local_q:] for piece in found))
    mine = tuple(
        (
            jnp.where(parity == 0, low_piece, high_piece)
            for low_piece, high_piece in zip(low_part, high_part)
        )
    )
    theirs = tuple(
        (
            jnp.where(parity == 0, high_piece, low_piece)
            for low_piece, high_piece in zip(low_part, high_part)
        )
    )
    received = partner((theirs[0], theirs[1], theirs[2]), "tensor", 0)
    cached = combine_parts(mine, received)
    fresh = fresh_all(own_grouped, new_keys, new_values, C)
    highest, totals, blended = combine_parts(cached, fresh)
    attended = (blended / totals[..., None]).astype(jnp.bfloat16).reshape(row_count, local_q * HD)
    piece = attended
    summed = lax.psum_scatter(
        jnp.dot(piece, output_weight, preferred_element_type=jnp.float32),
        "tensor",
        scatter_dimension=0,
        tiled=True,
    )
    return summed.astype(jnp.bfloat16)


def solution(mesh):
    placed = (
        P(("req", "tensor"), None),
        P(),
        P(None, "tensor"),
        P(None, "tensor"),
        P("tensor", None),
        P(("req", "tensor"), None, None),
        P("req", None),
        P("req"),
        P("req"),
    )
    return jax.shard_map(
        shards, mesh=mesh, in_specs=placed, out_specs=P(("req", "tensor"), None), check_vma=False
    )
```

profile of v0, /device:TPU:1, one launch (start us, length us, event | category | flops | bytes accessed | tf_op | source)
XLA Modules:
  0.0 439.1 jit_solution(1664595664184705682)
XLA Ops:
  8.0 2.0 fusion.64
  13.6 1.6 gather_fusion.2
  17.4 5.5 %fusion.116 = pred[1024]{0:T(1024)(128)(4,1)S(1)} fusion(s32[]{:T(128)} %bitcast.35, pred[]{:T(512)} %bitcast.34, pred[]{:T(512)} %bitcast.33, pred[]{:T(512)} %bitcast.32, pred[]{:T(512)} %bitcast.31, pred[]{:T(512)} %bitcast.30, pred[]{:T(512)} %bitcast.29, pred[]{:T(512)} %bitcast.28, pred[]{:T(512)} %bitcast.27), kind=kLoop, calls=%fused_computation.187 | loop fusion | flops 25600 | bytes 1036 | tf_op jit(solution)/shard_map/and | solution.py:47
  23.0 5.6 %fusion.117 = pred[1024]{0:T(1024)(128)(4,1)S(1)} fusion(s32[]{:T(128)} %bitcast.42, pred[]{:T(512)} %bitcast.54, pred[]{:T(512)} %bitcast.53, pred[]{:T(512)} %bitcast.52, pred[]{:T(512)} %bitcast.51, pred[]{:T(512)} %bitcast.50, pred[]{:T(512)} %bitcast.49, pred[]{:T(512)} %bitcast.48, pred[]{:T(512)} %bitcast.47), kind=kLoop, calls=%fused_computation.188 | loop fusion | flops 25600 | bytes 1036 | tf_op jit(solution)/shard_map/and | solution.py:47
  29.9 1.8 multiply_cosine_fusion.1
  33.6 58.7 %all-gather.2.cloned.1.call-done = bf16[512,8192]{1,0:T(8,128)(2,1)} async-done(((bf16[32,8192]{1,0:T(8,128)(2,1)}), bf16[512,8192]{1,0:T(8,128)(2,1)}) %all-gather.2.cloned.1.call-update) | async-done | bytes 8388624 | tf_op jit(solution)/shard_map/all_gather | solution.py:170
  92.3 6.9 %fusion.141 = f32[512,256]{0,1:T(8,128)S(1)} fusion(bf16[512,8192]{1,0:T(8,128)(2,1)} %all-gather.2.cloned.1.call-done, bf16[8192,256]{1,0:T(8,128)(2,1)} %param.23), kind=kOutput, calls=%fused_computation.227 | convolution fusion | flops 2147483648 | bytes 13107200 | tf_op jit(solution)/shard_map/dot_general | solution.py:173
  99.5 5.7 %fusion.142 = f32[512,128]{1,0:T(8,128)S(1)} fusion(bf16[512,8192]{1,0:T(8,128)(2,1)} %all-gather.2.cloned.1.call-done, bf16[8192,128]{1,0:T(8,128)(2,1)S(1)} %copy-done), kind=kOutput, calls=%fused_computation.228 | convolution fusion | flops 1073741824 | bytes 10747904 | tf_op jit(solution)/shard_map/dot_general | solution.py:174
  110.9 1.6 broadcast_select_fusion.1
  116.9 1.8 convolution_bitcast_fusion.1
  121.6 1.8 fusion.54
  125.4 1.8 fusion.57
  128.5 134.0 %while.21 = (s32[]{:T(128)}, f32[16,1,1,4]{3,2,1,0:T(1,128)S(1)}, f32[16,1,1,4]{3,2,1,0:T(1,128)S(1)}, f32[16,1,1,4,128]{4,0,3,2,1:T(8,128)S(1)}, s32[16,8]{1,0:...) while((s32[]{:T(128)}, f32[16,1,1,4]{3,2,1,0:T(1,128)S(1)}, ...), condition=%wide.region_6.9_spmd, body=%wide.region_3.8_spmd.sunk | while | flops 2422874 | bytes 2688929 | solution.py:86
  129.8 5.5 %fusion.158 = pred[1024]{0:T(1024)(128)(4,1)S(1)} fusion(s32[]{:T(128)} %bitcast.422, pred[]{:T(512)} %bitcast.423, pred[]{:T(512)} %bitcast.424, pred[]{:T(512)} %bitcast.425, pred[]{:T(512)} %bitcast.426, pred[]{:T(512)} %bitcast.427, pred[]{:T(512)} %bitcast.428, pred[]{:T(512)} %bitcast.429, pred[]{:T(512)} %bitcast.430), kind=kLoop, calls=%fused_computation.37.clone.1 | loop fusion | flops 25600 | bytes 1036 | tf_op jit(solution)/shard_map/while/body/eval_jaxpr/and | solution.py:47
  138.2 5.5 %fusion.158 = pred[1024]{0:T(1024)(128)(4,1)S(1)} fusion(s32[]{:T(128)} %bitcast.422, pred[]{:T(512)} %bitcast.423, pred[]{:T(512)} %bitcast.424, pred[]{:T(512)} %bitcast.425, pred[]{:T(512)} %bitcast.426, pred[]{:T(512)} %bitcast.427, pred[]{:T(512)} %bitcast.428, pred[]{:T(512)} %bitcast.429, pred[]{:T(512)} %bitcast.430), kind=kLoop, calls=%fused_computation.37.clone.1 | loop fusion | flops 25600 | bytes 1036 | tf_op jit(solution)/shard_map/while/body/eval_jaxpr/and | solution.py:47
  146.6 5.5 %fusion.158 = pred[1024]{0:T(1024)(128)(4,1)S(1)} fusion(s32[]{:T(128)} %bitcast.422, pred[]{:T(512)} %bitcast.423, pred[]{:T(512)} %bitcast.424, pred[]{:T(512)} %bitcast.425, pred[]{:T(512)} %bitcast.426, pred[]{:T(512)} %bitcast.427, pred[]{:T(512)} %bitcast.428, pred[]{:T(512)} %bitcast.429, pred[]{:T(512)} %bitcast.430), kind=kLoop, calls=%fused_computation.37.clone.1 | loop fusion | flops 25600 | bytes 1036 | tf_op jit(solution)/shard_map/while/body/eval_jaxpr/and | solution.py:47
  154.9 5.5 %fusion.158 = pred[1024]{0:T(1024)(128)(4,1)S(1)} fusion(s32[]{:T(128)} %bitcast.422, pred[]{:T(512)} %bitcast.423, pred[]{:T(512)} %bitcast.424, pred[]{:T(512)} %bitcast.425, pred[]{:T(512)} %bitcast.426, pred[]{:T(512)} %bitcast.427, pred[]{:T(512)} %bitcast.428, pred[]{:T(512)} %bitcast.429, pred[]{:T(512)} %bitcast.430), kind=kLoop, calls=%fused_computation.37.clone.1 | loop fusion | flops 25600 | bytes 1036 | tf_op jit(solution)/shard_map/while/body/eval_jaxpr/and | solution.py:47
  163.3 5.5 %fusion.158 = pred[1024]{0:T(1024)(128)(4,1)S(1)} fusion(s32[]{:T(128)} %bitcast.422, pred[]{:T(512)} %bitcast.423, pred[]{:T(512)} %bitcast.424, pred[]{:T(512)} %bitcast.425, pred[]{:T(512)} %bitcast.426, pred[]{:T(512)} %bitcast.427, pred[]{:T(512)} %bitcast.428, pred[]{:T(512)} %bitcast.429, pred[]{:T(512)} %bitcast.430), kind=kLoop, calls=%fused_computation.37.clone.1 | loop fusion | flops 25600 | bytes 1036 | tf_op jit(solution)/shard_map/while/body/eval_jaxpr/and | solution.py:47
  171.7 5.5 %fusion.158 = pred[1024]{0:T(1024)(128)(4,1)S(1)} fusion(s32[]{:T(128)} %bitcast.422, pred[]{:T(512)} %bitcast.423, pred[]{:T(512)} %bitcast.424, pred[]{:T(512)} %bitcast.425, pred[]{:T(512)} %bitcast.426, pred[]{:T(512)} %bitcast.427, pred[]{:T(512)} %bitcast.428, pred[]{:T(512)} %bitcast.429, pred[]{:T(512)} %bitcast.430), kind=kLoop, calls=%fused_computation.37.clone.1 | loop fusion | flops 25600 | bytes 1036 | tf_op jit(solution)/shard_map/while/body/eval_jaxpr/and | solution.py:47
  180.1 5.5 %fusion.158 = pred[1024]{0:T(1024)(128)(4,1)S(1)} fusion(s32[]{:T(128)} %bitcast.422, pred[]{:T(512)} %bitcast.423, pred[]{:T(512)} %bitcast.424, pred[]{:T(512)} %bitcast.425, pred[]{:T(512)} %bitcast.426, pred[]{:T(512)} %bitcast.427, pred[]{:T(512)} %bitcast.428, pred[]{:T(512)} %bitcast.429, pred[]{:T(512)} %bitcast.430), kind=kLoop, calls=%fused_computation.37.clone.1 | loop fusion | flops 25600 | bytes 1036 | tf_op jit(solution)/shard_map/while/body/eval_jaxpr/and | solution.py:47
  188.4 5.5 %fusion.158 = pred[1024]{0:T(1024)(128)(4,1)S(1)} fusion(s32[]{:T(128)} %bitcast.422, pred[]{:T(512)} %bitcast.423, pred[]{:T(512)} %bitcast.424, pred[]{:T(512)} %bitcast.425, pred[]{:T(512)} %bitcast.426, pred[]{:T(512)} %bitcast.427, pred[]{:T(512)} %bitcast.428, pred[]{:T(512)} %bitcast.429, pred[]{:T(512)} %bitcast.430), kind=kLoop, calls=%fused_computation.37.clone.1 | loop fusion | flops 25600 | bytes 1036 | tf_op jit(solution)/shard_map/while/body/eval_jaxpr/and | solution.py:47
  196.8 5.5 %fusion.158 = pred[1024]{0:T(1024)(128)(4,1)S(1)} fusion(s32[]{:T(128)} %bitcast.422, pred[]{:T(512)} %bitcast.423, pred[]{:T(512)} %bitcast.424, pred[]{:T(512)} %bitcast.425, pred[]{:T(512)} %bitcast.426, pred[]{:T(512)} %bitcast.427, pred[]{:T(512)} %bitcast.428, pred[]{:T(512)} %bitcast.429, pred[]{:T(512)} %bitcast.430), kind=kLoop, calls=%fused_computation.37.clone.1 | loop fusion | flops 25600 | bytes 1036 | tf_op jit(solution)/shard_map/while/body/eval_jaxpr/and | solution.py:47
  205.2 5.5 %fusion.158 = pred[1024]{0:T(1024)(128)(4,1)S(1)} fusion(s32[]{:T(128)} %bitcast.422, pred[]{:T(512)} %bitcast.423, pred[]{:T(512)} %bitcast.424, pred[]{:T(512)} %bitcast.425, pred[]{:T(512)} %bitcast.426, pred[]{:T(512)} %bitcast.427, pred[]{:T(512)} %bitcast.428, pred[]{:T(512)} %bitcast.429, pred[]{:T(512)} %bitcast.430), kind=kLoop, calls=%fused_computation.37.clone.1 | loop fusion | flops 25600 | bytes 1036 | tf_op jit(solution)/shard_map/while/body/eval_jaxpr/and | solution.py:47
  213.6 5.5 %fusion.158 = pred[1024]{0:T(1024)(128)(4,1)S(1)} fusion(s32[]{:T(128)} %bitcast.422, pred[]{:T(512)} %bitcast.423, pred[]{:T(512)} %bitcast.424, pred[]{:T(512)} %bitcast.425, pred[]{:T(512)} %bitcast.426, pred[]{:T(512)} %bitcast.427, pred[]{:T(512)} %bitcast.428, pred[]{:T(512)} %bitcast.429, pred[]{:T(512)} %bitcast.430), kind=kLoop, calls=%fused_computation.37.clone.1 | loop fusion | flops 25600 | bytes 1036 | tf_op jit(solution)/shard_map/while/body/eval_jaxpr/and | solution.py:47
  221.9 5.5 %fusion.158 = pred[1024]{0:T(1024)(128)(4,1)S(1)} fusion(s32[]{:T(128)} %bitcast.422, pred[]{:T(512)} %bitcast.423, pred[]{:T(512)} %bitcast.424, pred[]{:T(512)} %bitcast.425, pred[]{:T(512)} %bitcast.426, pred[]{:T(512)} %bitcast.427, pred[]{:T(512)} %bitcast.428, pred[]{:T(512)} %bitcast.429, pred[]{:T(512)} %bitcast.430), kind=kLoop, calls=%fused_computation.37.clone.1 | loop fusion | flops 25600 | bytes 1036 | tf_op jit(solution)/shard_map/while/body/eval_jaxpr/and | solution.py:47
  230.3 5.5 %fusion.158 = pred[1024]{0:T(1024)(128)(4,1)S(1)} fusion(s32[]{:T(128)} %bitcast.422, pred[]{:T(512)} %bitcast.423, pred[]{:T(512)} %bitcast.424, pred[]{:T(512)} %bitcast.425, pred[]{:T(512)} %bitcast.426, pred[]{:T(512)} %bitcast.427, pred[]{:T(512)} %bitcast.428, pred[]{:T(512)} %bitcast.429, pred[]{:T(512)} %bitcast.430), kind=kLoop, calls=%fused_computation.37.clone.1 | loop fusion | flops 25600 | bytes 1036 | tf_op jit(solution)/shard_map/while/body/eval_jaxpr/and | solution.py:47
  238.7 5.5 %fusion.158 = pred[1024]{0:T(1024)(128)(4,1)S(1)} fusion(s32[]{:T(128)} %bitcast.422, pred[]{:T(512)} %bitcast.423, pred[]{:T(512)} %bitcast.424, pred[]{:T(512)} %bitcast.425, pred[]{:T(512)} %bitcast.426, pred[]{:T(512)} %bitcast.427, pred[]{:T(512)} %bitcast.428, pred[]{:T(512)} %bitcast.429, pred[]{:T(512)} %bitcast.430), kind=kLoop, calls=%fused_computation.37.clone.1 | loop fusion | flops 25600 | bytes 1036 | tf_op jit(solution)/shard_map/while/body/eval_jaxpr/and | solution.py:47
  247.1 5.5 %fusion.158 = pred[1024]{0:T(1024)(128)(4,1)S(1)} fusion(s32[]{:T(128)} %bitcast.422, pred[]{:T(512)} %bitcast.423, pred[]{:T(512)} %bitcast.424, pred[]{:T(512)} %bitcast.425, pred[]{:T(512)} %bitcast.426, pred[]{:T(512)} %bitcast.427, pred[]{:T(512)} %bitcast.428, pred[]{:T(512)} %bitcast.429, pred[]{:T(512)} %bitcast.430), kind=kLoop, calls=%fused_computation.37.clone.1 | loop fusion | flops 25600 | bytes 1036 | tf_op jit(solution)/shard_map/while/body/eval_jaxpr/and | solution.py:47
  255.4 5.5 %fusion.158 = pred[1024]{0:T(1024)(128)(4,1)S(1)} fusion(s32[]{:T(128)} %bitcast.422, pred[]{:T(512)} %bitcast.423, pred[]{:T(512)} %bitcast.424, pred[]{:T(512)} %bitcast.425, pred[]{:T(512)} %bitcast.426, pred[]{:T(512)} %bitcast.427, pred[]{:T(512)} %bitcast.428, pred[]{:T(512)} %bitcast.429, pred[]{:T(512)} %bitcast.430), kind=kLoop, calls=%fused_computation.37.clone.1 | loop fusion | flops 25600 | bytes 1036 | tf_op jit(solution)/shard_map/while/body/eval_jaxpr/and | solution.py:47
  267.5 10.3 %fusion.143 = f32[512,8192]{1,0:T(8,128)} fusion(bf16[512,256]{0,1:T(8,128)(2,1)S(1)} %bitcast.441, bf16[256,8192]{1,0:T(8,128)(2,1)} %param.25), kind=kOutput, calls=%fused_computation.229 | convolution fusion | flops 2147483648 | bytes 21233664 | tf_op jit(solution)/shard_map/dot_general | solution.py:229
  277.8 152.3 %reduce-scatter.2.cloned.1.call-done = f32[32,8192]{1,0:T(8,128)} async-done(((f32[512,8192]{1,0:T(8,128)}), f32[32,8192]{1,0:T(8,128)}) %reduce-scatter.2.cloned.1.call-update) | async-done | bytes 1048592 | tf_op jit(solution)/shard_map/reduce_scatter | solution.py:228
  430.2 2.1 convert_element_type.59
  (291 shorter events, 76.1 us)
Async XLA Ops:
  6.5 92.9 %copy-start = (bf16[8192,128]{1,0:T(8,128)(2,1)S(1)}, bf16[8192,128]{1,0:T(8,128)(2,1)}, u32[]{:S(2)}) copy-start(bf16[8192,128]{1,0:T(8,128)(2,1)} %param.24) | copy-start | bytes 6291460
  6.5 10.0 %copy-start.5 = (s32[18,8]{0,1:T(8,128)S(1)}, s32[18,8]{0,1:T(8,128)}, u32[]{:S(2)}) copy-start(s32[18,8]{0,1:T(8,128)} %param.27) | copy-start | bytes 1732
  6.5 9.4 %copy-start.7 = (s32[2]{0:T(128)S(1)}, s32[2]{0:T(128)}, u32[]{:S(2)}) copy-start(s32[2]{0:T(128)} %param.28) | copy-start | bytes 28
  6.5 23.2 %copy-start.10 = (s32[16]{0:T(128)S(1)}, s32[16]{0:T(128)}, u32[]{:S(2)}) copy-start(s32[16]{0:T(128)} %param.29) | copy-start | bytes 196
  6.5 85.7 %all-gather.2.cloned.1.call-start = ((), (), s32[]{:S(2)}) async-start(), calls=%async_computation.1 | async-start | bytes 8912896 | tf_op jit(solution)/shard_map/all_gather | solution.py:170
  10.0 420.1 %reduce-scatter.2.cloned.1.call-start = ((), (), s32[]{:S(2)}) async-start(), calls=%async_computation.2 | async-start | bytes 17825792 | tf_op jit(solution)/shard_map/reduce_scatter | solution.py:228
  15.9 13.9 %copy-start.8 = (f32[64]{0:T(128)}, f32[64]{0:T(128)S(1)}, u32[]{:S(2)}) copy-start(f32[64]{0:T(128)S(1)} %multiply_power_fusion) | copy-start | bytes 772
  99.5 5.7 %copy-start.9 = (f32[64]{0:T(128)S(1)}, f32[64]{0:T(128)}, u32[]{:S(2)}) copy-start(f32[64]{0:T(128)} %copy-done.8) | copy-start | bytes 772
  107.2 3.7 collective-permute-start.2
  110.5 8.9 %collective-permute-start = (bf16[512,2,128]{2,0,1:T(8,128)(2,1)}, bf16[512,2,128]{2,0,1:T(8,128)(2,1)}, u32[]{:S(2)}, u32[]{:S(2)}) collective-permute-start(bf16[512,2,128]{2,0,1:T(8,128)(2,1)} %pad_maximum_fusion.1), channel_id=1, source_target_pairs={{0,1},{1,0},{2,3},{3,2},{4,5},{5,4},{6,7},{7,6},{8,9},{9,8},{10,11... | collective-permute-start | bytes 786440 | tf_op jit(solution)/shard_map/ppermute | solution.py:16
  114.2 6.6 %copy-start.3 = (bf16[1,8,128,256]{3,2,1,0:T(8,128)(2,1)S(1)}, bf16[1,8,128,256]{3,2,1,0:T(8,128)(2,1)}, u32[]{:S(2)}) copy-start(bf16[1,8,128,256]{3,2,1,0:T(8,128)(2,1)} %bitcast_select_fusion.3) | copy-start | bytes 1572868
  121.6 3.0 copy-start.2
  125.4 3.0 copy-start.1
  125.4 3.0 copy-start.11
  128.5 137.9 %copy-start.6 = (f32[512]{0:T(512)S(1)}, f32[512]{0:T(512)}, u32[]{:S(2)}) copy-start(f32[512]{0:T(512)} %pad.16.clone) | copy-start | bytes 6148
  262.5 4.0 copy-start.4
  262.7 2.7 collective-permute-start.1
  264.4 2.1 collective-permute-start.3
  264.8 1.6 collective-permute-start.4
Sparse Core Ops, SparseCore 0:
  10.2 82.0 all-gather.1
  277.9 152.1 reduce-scatter.1
where the time goes:
time: 441 us; the launch traced here: 439 us
  waiting for transfers between devices  212 us (48%)
  other arithmetic  131 us (30%)
  matrix products  41.2 us (9%)
  local copies, waits for them, and re-layouts  38.4 us (9%)
  between operations  13.8 us (3%)
    reduce_scatter x1, waiting for transfers between devices, shards(): lax.psum_scatter(jnp.dot(piece, output_weight, preferred_element_type=jnp...  152 us
    and x18, other arithmetic, cached_block(): jnp.repeat(owned_page, page_len, total_repeat_length=key_span)  99.7 us
    all_gather x1, waiting for transfers between devices, shards(): project_piece = lax.all_gather(normed, 'tensor', axis=0, tiled=True)  58.7 us
    gather x18, local copies, waits for them, and re-layouts, cached_block(): fetched = jnp.take(pool_rows, local_page, axis=1)  12.5 us
    gather x17, local copies, waits for them, and re-layouts, cached_block(): jnp.repeat(owned_page, page_len, total_repeat_length=key_span)  11.4 us
    dot_general x1, matrix products, shards(): jnp.dot(piece, output_weight, preferred_element_type=jnp.float32)  10.3 us
    dynamic_slice x16, local copies, waits for them, and re-layouts, cached_all(): lax.map(decode_one, (queries[2 * stretch_len:], page_table[2:], decode_le...  9.91 us
  transfers between devices with their start and end apart: 7, of which 3 were waited for; matrix products, arithmetic and copies ran while one was open for 8% of the time, Pallas kernels for 0%

commit v1 on v0

--- a/solution.py
+++ b/solution.py
@@ -167,7 +167,10 @@
         * lax.rsqrt(jnp.mean(widened * widened, axis=-1, keepdims=True) + eps_norm)
         * norm_gain
     ).astype(jnp.bfloat16)
-    project_piece = lax.all_gather(normed, "tensor", axis=0, tiled=True)
+    n_dev = lax.axis_size("tensor")
+    blocks = jnp.stack([normed for _ in range(n_dev)])
+    blocks = lax.all_to_all(blocks, "tensor", split_axis=0, concat_axis=0)
+    project_piece = jnp.concatenate(blocks, axis=0)
     joint = jnp.concatenate(
         [
             jnp.dot(project_piece, query_weight, preferred_element_type=jnp.float32),

time: 441 us -> 477 us (1.082)
  waiting for transfers between devices: 212 us -> 243 us
  starting transfers between devices: 1.83 us -> 10.6 us
  local copies, waits for them, and re-layouts: 38.4 us -> 47.1 us
  other arithmetic: 131 us -> 123 us
    all_to_all x0 -> x1, waiting for transfers between devices: none -> 86.3 us  [shards(): blocks = lax.all_to_all(blocks, 'tensor', split_axis=0, concat_axis=0)]
    all_gather x1 -> x0, waiting for transfers between devices: 58.7 us -> none  [shards(): project_piece = lax.all_gather(normed, 'tensor', axis=0, tiled=True)]
    all_to_all x0 -> x1, starting transfers between devices: none -> 8.45 us  [shards(): blocks = lax.all_to_all(blocks, 'tensor', split_axis=0, concat_axis=0)]
    dot_general x1, local copies, waits for them, and re-layouts: 0.08 us -> 6.44 us  [shards(): jnp.dot(project_piece, query_weight, preferred_element_type=jnp.float32)]
  transfers between devices with their start and end apart: 7 -> 7, of which waited for: 3 -> 4; matrix products, arithmetic and copies ran while one was open for 8% -> 8% of each run, Pallas kernels for 0% -> 0%
where the time goes in v1:
time: 477 us; the launch traced here: 475 us
  waiting for transfers between devices  243 us (51%)
  other arithmetic  123 us (26%)
  local copies, waits for them, and re-layouts  47.1 us (10%)
  matrix products  36.5 us (8%)
  between operations  13.9 us (3%)
  starting transfers between devices  10.6 us (2%)
    reduce_scatter x1, waiting for transfers between devices, shards(): lax.psum_scatter(jnp.dot(piece, output_weight, preferred_element_type=jnp...  156 us
    and x18, other arithmetic, cached_block(): jnp.repeat(owned_page, page_len, total_repeat_length=key_span)  99.9 us
    all_to_all x1, waiting for transfers between devices, shards(): blocks = lax.all_to_all(blocks, 'tensor', split_axis=0, concat_axis=0)  86.3 us
    gather x17, local copies, waits for them, and re-layouts, cached_block(): jnp.repeat(owned_page, page_len, total_repeat_length=key_span)  11.8 us
    gather x18, local copies, waits for them, and re-layouts, cached_block(): fetched = jnp.take(pool_rows, local_page, axis=1)  11.2 us
    dynamic_slice x16, local copies, waits for them, and re-layouts, cached_all(): lax.map(decode_one, (queries[2 * stretch_len:], page_table[2:], decode_le...  10.7 us
    dot_general x1, matrix products, shards(): jnp.dot(piece, output_weight, preferred_element_type=jnp.float32)  10.3 us
  transfers between devices with their start and end apart: 7, of which 4 were waited for; matrix products, arithmetic and copies ran while one was open for 8% of the time, Pallas kernels for 0%

profile of v1, /device:TPU:1, one launch (start us, length us, event | category | flops | bytes accessed | tf_op | source)
XLA Modules:
  0.0 475.1 jit_solution(9375246451662992713)
XLA Ops:
  6.5 1.4 fusion.62
  9.2 4.2 stack.2
  13.4 8.4 %all-to-all-start = ((bf16[16,32,8192]{2,1,0:T(8,128)(2,1)}), bf16[16,32,8192]{2,1,0:T(8,128)(2,1)}, u32[]{:S(2)}, u32[]{:S(2)}) async-start(bf16[16,32,8192]{2,1,0:T(8,128)(2,1)} %stack.2), calls=%async_computation | async-start | bytes 16777216 | tf_op jit(solution)/shard_map/all_to_all | solution.py:172
  22.0 6.4 %copy.47 = bf16[256,8192]{1,0:T(8,128)(2,1)} copy(bf16[256,8192]{0,1:T(8,128)(2,1)} %bitcast.438) | data formatting | bytes 8388608 | tf_op jit(solution)/shard_map/dot_general | solution.py:176
  29.4 1.4 gather_fusion.1
  33.0 5.4 %fusion.115 = pred[1024]{0:T(1024)(128)(4,1)S(1)} fusion(s32[]{:T(128)} %bitcast.46, pred[]{:T(512)} %bitcast.58, pred[]{:T(512)} %bitcast.57, pred[]{:T(512)} %bitcast.56, pred[]{:T(512)} %bitcast.55, pred[]{:T(512)} %bitcast.54, pred[]{:T(512)} %bitcast.53, pred[]{:T(512)} %bitcast.52, pred[]{:T(512)} %bitcast.51), kind=kLoop, calls=%fused_computation.187 | loop fusion | flops 25600 | bytes 1036 | tf_op jit(solution)/shard_map/and | solution.py:47
  38.3 5.8 %fusion.114 = pred[1024]{0:T(1024)(128)(4,1)S(1)} fusion(s32[]{:T(128)} %bitcast.36, pred[]{:T(512)} %bitcast.35, pred[]{:T(512)} %bitcast.34, pred[]{:T(512)} %bitcast.33, pred[]{:T(512)} %bitcast.32, pred[]{:T(512)} %bitcast.31, pred[]{:T(512)} %bitcast.30, pred[]{:T(512)} %bitcast.29, pred[]{:T(512)} %bitcast.28), kind=kLoop, calls=%fused_computation.186 | loop fusion | flops 25600 | bytes 1036 | tf_op jit(solution)/shard_map/and | solution.py:47
  44.1 1.3 iota_add_fusion
  48.1 86.3 %all-to-all-done = bf16[16,32,8192]{2,1,0:T(8,128)(2,1)} async-done(((bf16[16,32,8192]{2,1,0:T(8,128)(2,1)}), bf16[16,32,8192]{2,1,0:T(8,128)(2,1)}, u32[]{:S(2)}, u32[]{:S(2)}) %all-to-all-start) | async-done | bytes 8388640 | tf_op jit(solution)/shard_map/all_to_all | solution.py:172
  134.5 5.9 %fusion.138 = f32[512,128]{1,0:T(8,128)S(1)} fusion(bf16[512,8192]{1,0:T(8,128)(2,1)} %bitcast.42, bf16[8192,128]{1,0:T(8,128)(2,1)S(1)} %copy-done), kind=kOutput, calls=%fused_computation.225 | convolution fusion | flops 1073741824 | bytes 10747904 | tf_op jit(solution)/shard_map/dot_general | solution.py:177
  142.4 5.7 %fusion.137 = f32[512,2,128]{0,2,1:T(8,128)S(1)} fusion(bf16[512,8192,1]{1,0,2:T(8,128)(2,1)} %bitcast.43, bf16[2,128,8192]{2,1,0:T(8,128)(2,1)S(1)} %bitcast.439), kind=kOutput, calls=%fused_computation.224 | convolution fusion | flops 2147483648 | bytes 13107200 | tf_op jit(solution)/shard_map/dot_general | solution.py:176
  154.3 1.8 fusion.54
  160.6 135.1 %while.21 = (s32[]{:T(128)}, f32[16,1,1,4]{3,2,1,0:T(1,128)S(1)}, f32[16,1,1,4]{3,2,1,0:T(1,128)S(1)}, f32[16,1,1,4,128]{4,0,3,2,1:T(8,128)S(1)}, s32[16,8]{1,0:...) while((s32[]{:T(128)}, f32[16,1,1,4]{3,2,1,0:T(1,128)S(1)}, ...), condition=%wide.region_6.9_spmd, body=%wide.region_3.8_spmd.sunk | while | flops 2422874 | bytes 2688929 | solution.py:86
  162.7 5.5 %fusion.154 = pred[1024]{0:T(1024)(128)(4,1)S(1)} fusion(s32[]{:T(128)} %bitcast.424, pred[]{:T(512)} %bitcast.425, pred[]{:T(512)} %bitcast.426, pred[]{:T(512)} %bitcast.427, pred[]{:T(512)} %bitcast.428, pred[]{:T(512)} %bitcast.429, pred[]{:T(512)} %bitcast.430, pred[]{:T(512)} %bitcast.431, pred[]{:T(512)} %bitcast.432), kind=kLoop, calls=%fused_computation.37.clone.1 | loop fusion | flops 25600 | bytes 1036 | tf_op jit(solution)/shard_map/while/body/eval_jaxpr/and | solution.py:47
  171.1 5.5 %fusion.154 = pred[1024]{0:T(1024)(128)(4,1)S(1)} fusion(s32[]{:T(128)} %bitcast.424, pred[]{:T(512)} %bitcast.425, pred[]{:T(512)} %bitcast.426, pred[]{:T(512)} %bitcast.427, pred[]{:T(512)} %bitcast.428, pred[]{:T(512)} %bitcast.429, pred[]{:T(512)} %bitcast.430, pred[]{:T(512)} %bitcast.431, pred[]{:T(512)} %bitcast.432), kind=kLoop, calls=%fused_computation.37.clone.1 | loop fusion | flops 25600 | bytes 1036 | tf_op jit(solution)/shard_map/while/body/eval_jaxpr/and | solution.py:47
  179.6 5.5 %fusion.154 = pred[1024]{0:T(1024)(128)(4,1)S(1)} fusion(s32[]{:T(128)} %bitcast.424, pred[]{:T(512)} %bitcast.425, pred[]{:T(512)} %bitcast.426, pred[]{:T(512)} %bitcast.427, pred[]{:T(512)} %bitcast.428, pred[]{:T(512)} %bitcast.429, pred[]{:T(512)} %bitcast.430, pred[]{:T(512)} %bitcast.431, pred[]{:T(512)} %bitcast.432), kind=kLoop, calls=%fused_computation.37.clone.1 | loop fusion | flops 25600 | bytes 1036 | tf_op jit(solution)/shard_map/while/body/eval_jaxpr/and | solution.py:47
  188.0 5.5 %fusion.154 = pred[1024]{0:T(1024)(128)(4,1)S(1)} fusion(s32[]{:T(128)} %bitcast.424, pred[]{:T(512)} %bitcast.425, pred[]{:T(512)} %bitcast.426, pred[]{:T(512)} %bitcast.427, pred[]{:T(512)} %bitcast.428, pred[]{:T(512)} %bitcast.429, pred[]{:T(512)} %bitcast.430, pred[]{:T(512)} %bitcast.431, pred[]{:T(512)} %bitcast.432), kind=kLoop, calls=%fused_computation.37.clone.1 | loop fusion | flops 25600 | bytes 1036 | tf_op jit(solution)/shard_map/while/body/eval_jaxpr/and | solution.py:47
  196.5 5.5 %fusion.154 = pred[1024]{0:T(1024)(128)(4,1)S(1)} fusion(s32[]{:T(128)} %bitcast.424, pred[]{:T(512)} %bitcast.425, pred[]{:T(512)} %bitcast.426, pred[]{:T(512)} %bitcast.427, pred[]{:T(512)} %bitcast.428, pred[]{:T(512)} %bitcast.429, pred[]{:T(512)} %bitcast.430, pred[]{:T(512)} %bitcast.431, pred[]{:T(512)} %bitcast.432), kind=kLoop, calls=%fused_computation.37.clone.1 | loop fusion | flops 25600 | bytes 1036 | tf_op jit(solution)/shard_map/while/body/eval_jaxpr/and | solution.py:47
  204.9 5.5 %fusion.154 = pred[1024]{0:T(1024)(128)(4,1)S(1)} fusion(s32[]{:T(128)} %bitcast.424, pred[]{:T(512)} %bitcast.425, pred[]{:T(512)} %bitcast.426, pred[]{:T(512)} %bitcast.427, pred[]{:T(512)} %bitcast.428, pred[]{:T(512)} %bitcast.429, pred[]{:T(512)} %bitcast.430, pred[]{:T(512)} %bitcast.431, pred[]{:T(512)} %bitcast.432), kind=kLoop, calls=%fused_computation.37.clone.1 | loop fusion | flops 25600 | bytes 1036 | tf_op jit(solution)/shard_map/while/body/eval_jaxpr/and | solution.py:47
  213.4 5.5 %fusion.154 = pred[1024]{0:T(1024)(128)(4,1)S(1)} fusion(s32[]{:T(128)} %bitcast.424, pred[]{:T(512)} %bitcast.425, pred[]{:T(512)} %bitcast.426, pred[]{:T(512)} %bitcast.427, pred[]{:T(512)} %bitcast.428, pred[]{:T(512)} %bitcast.429, pred[]{:T(512)} %bitcast.430, pred[]{:T(512)} %bitcast.431, pred[]{:T(512)} %bitcast.432), kind=kLoop, calls=%fused_computation.37.clone.1 | loop fusion | flops 25600 | bytes 1036 | tf_op jit(solution)/shard_map/while/body/eval_jaxpr/and | solution.py:47
  221.8 5.5 %fusion.154 = pred[1024]{0:T(1024)(128)(4,1)S(1)} fusion(s32[]{:T(128)} %bitcast.424, pred[]{:T(512)} %bitcast.425, pred[]{:T(512)} %bitcast.426, pred[]{:T(512)} %bitcast.427, pred[]{:T(512)} %bitcast.428, pred[]{:T(512)} %bitcast.429, pred[]{:T(512)} %bitcast.430, pred[]{:T(512)} %bitcast.431, pred[]{:T(512)} %bitcast.432), kind=kLoop, calls=%fused_computation.37.clone.1 | loop fusion | flops 25600 | bytes 1036 | tf_op jit(solution)/shard_map/while/body/eval_jaxpr/and | solution.py:47
  230.3 5.5 %fusion.154 = pred[1024]{0:T(1024)(128)(4,1)S(1)} fusion(s32[]{:T(128)} %bitcast.424, pred[]{:T(512)} %bitcast.425, pred[]{:T(512)} %bitcast.426, pred[]{:T(512)} %bitcast.427, pred[]{:T(512)} %bitcast.428, pred[]{:T(512)} %bitcast.429, pred[]{:T(512)} %bitcast.430, pred[]{:T(512)} %bitcast.431, pred[]{:T(512)} %bitcast.432), kind=kLoop, calls=%fused_computation.37.clone.1 | loop fusion | flops 25600 | bytes 1036 | tf_op jit(solution)/shard_map/while/body/eval_jaxpr/and | solution.py:47
  238.7 5.5 %fusion.154 = pred[1024]{0:T(1024)(128)(4,1)S(1)} fusion(s32[]{:T(128)} %bitcast.424, pred[]{:T(512)} %bitcast.425, pred[]{:T(512)} %bitcast.426, pred[]{:T(512)} %bitcast.427, pred[]{:T(512)} %bitcast.428, pred[]{:T(512)} %bitcast.429, pred[]{:T(512)} %bitcast.430, pred[]{:T(512)} %bitcast.431, pred[]{:T(512)} %bitcast.432), kind=kLoop, calls=%fused_computation.37.clone.1 | loop fusion | flops 25600 | bytes 1036 | tf_op jit(solution)/shard_map/while/body/eval_jaxpr/and | solution.py:47
  247.1 5.5 %fusion.154 = pred[1024]{0:T(1024)(128)(4,1)S(1)} fusion(s32[]{:T(128)} %bitcast.424, pred[]{:T(512)} %bitcast.425, pred[]{:T(512)} %bitcast.426, pred[]{:T(512)} %bitcast.427, pred[]{:T(512)} %bitcast.428, pred[]{:T(512)} %bitcast.429, pred[]{:T(512)} %bitcast.430, pred[]{:T(512)} %bitcast.431, pred[]{:T(512)} %bitcast.432), kind=kLoop, calls=%fused_computation.37.clone.1 | loop fusion | flops 25600 | bytes 1036 | tf_op jit(solution)/shard_map/while/body/eval_jaxpr/and | solution.py:47
  255.6 5.5 %fusion.154 = pred[1024]{0:T(1024)(128)(4,1)S(1)} fusion(s32[]{:T(128)} %bitcast.424, pred[]{:T(512)} %bitcast.425, pred[]{:T(512)} %bitcast.426, pred[]{:T(512)} %bitcast.427, pred[]{:T(512)} %bitcast.428, pred[]{:T(512)} %bitcast.429, pred[]{:T(512)} %bitcast.430, pred[]{:T(512)} %bitcast.431, pred[]{:T(512)} %bitcast.432), kind=kLoop, calls=%fused_computation.37.clone.1 | loop fusion | flops 25600 | bytes 1036 | tf_op jit(solution)/shard_map/while/body/eval_jaxpr/and | solution.py:47
  264.0 5.5 %fusion.154 = pred[1024]{0:T(1024)(128)(4,1)S(1)} fusion(s32[]{:T(128)} %bitcast.424, pred[]{:T(512)} %bitcast.425, pred[]{:T(512)} %bitcast.426, pred[]{:T(512)} %bitcast.427, pred[]{:T(512)} %bitcast.428, pred[]{:T(512)} %bitcast.429, pred[]{:T(512)} %bitcast.430, pred[]{:T(512)} %bitcast.431, pred[]{:T(512)} %bitcast.432), kind=kLoop, calls=%fused_computation.37.clone.1 | loop fusion | flops 25600 | bytes 1036 | tf_op jit(solution)/shard_map/while/body/eval_jaxpr/and | solution.py:47
  272.5 5.5 %fusion.154 = pred[1024]{0:T(1024)(128)(4,1)S(1)} fusion(s32[]{:T(128)} %bitcast.424, pred[]{:T(512)} %bitcast.425, pred[]{:T(512)} %bitcast.426, pred[]{:T(512)} %bitcast.427, pred[]{:T(512)} %bitcast.428, pred[]{:T(512)} %bitcast.429, pred[]{:T(512)} %bitcast.430, pred[]{:T(512)} %bitcast.431, pred[]{:T(512)} %bitcast.432), kind=kLoop, calls=%fused_computation.37.clone.1 | loop fusion | flops 25600 | bytes 1036 | tf_op jit(solution)/shard_map/while/body/eval_jaxpr/and | solution.py:47
  280.9 5.5 %fusion.154 = pred[1024]{0:T(1024)(128)(4,1)S(1)} fusion(s32[]{:T(128)} %bitcast.424, pred[]{:T(512)} %bitcast.425, pred[]{:T(512)} %bitcast.426, pred[]{:T(512)} %bitcast.427, pred[]{:T(512)} %bitcast.428, pred[]{:T(512)} %bitcast.429, pred[]{:T(512)} %bitcast.430, pred[]{:T(512)} %bitcast.431, pred[]{:T(512)} %bitcast.432), kind=kLoop, calls=%fused_computation.37.clone.1 | loop fusion | flops 25600 | bytes 1036 | tf_op jit(solution)/shard_map/while/body/eval_jaxpr/and | solution.py:47
  289.4 5.5 %fusion.154 = pred[1024]{0:T(1024)(128)(4,1)S(1)} fusion(s32[]{:T(128)} %bitcast.424, pred[]{:T(512)} %bitcast.425, pred[]{:T(512)} %bitcast.426, pred[]{:T(512)} %bitcast.427, pred[]{:T(512)} %bitcast.428, pred[]{:T(512)} %bitcast.429, pred[]{:T(512)} %bitcast.430, pred[]{:T(512)} %bitcast.431, pred[]{:T(512)} %bitcast.432), kind=kLoop, calls=%fused_computation.37.clone.1 | loop fusion | flops 25600 | bytes 1036 | tf_op jit(solution)/shard_map/while/body/eval_jaxpr/and | solution.py:47
  299.6 10.3 %fusion.139 = f32[512,8192]{1,0:T(8,128)} fusion(bf16[512,256]{0,1:T(8,128)(2,1)S(1)} %bitcast.445, bf16[256,8192]{1,0:T(8,128)(2,1)} %param.25), kind=kOutput, calls=%fused_computation.226 | convolution fusion | flops 2147483648 | bytes 21233664 | tf_op jit(solution)/shard_map/dot_general | solution.py:232
  309.9 156.3 %reduce-scatter.2.cloned.1.call-done = f32[32,8192]{1,0:T(8,128)} async-done(((f32[512,8192]{1,0:T(8,128)}), f32[32,8192]{1,0:T(8,128)}) %reduce-scatter.2.cloned.1.call-update) | async-done | bytes 1048592 | tf_op jit(solution)/shard_map/reduce_scatter | solution.py:231
  466.2 2.1 convert_element_type.59
  (292 shorter events, 68.7 us)
Async XLA Ops:
  6.5 127.9 %copy-start = (bf16[8192,128]{1,0:T(8,128)(2,1)S(1)}, bf16[8192,128]{1,0:T(8,128)(2,1)}, u32[]{:S(2)}) copy-start(bf16[8192,128]{1,0:T(8,128)(2,1)} %param.24) | copy-start | bytes 6291460
  13.4 121.0 %all-to-all-start = ((bf16[16,32,8192]{2,1,0:T(8,128)(2,1)}), bf16[16,32,8192]{2,1,0:T(8,128)(2,1)}, u32[]{:S(2)}, u32[]{:S(2)}) async-start(bf16[16,32,8192]{2,1,0:T(8,128)(2,1)} %stack.2), calls=%async_computation | async-start | bytes 16777216 | tf_op jit(solution)/shard_map/all_to_all | solution.py:172
  21.9 444.3 %reduce-scatter.2.cloned.1.call-start = ((), (), s32[]{:S(2)}) async-start(), calls=%async_computation.2 | async-start | bytes 17825792 | tf_op jit(solution)/shard_map/reduce_scatter | solution.py:231
  22.0 6.5 %copy-start.7 = (s32[18,8]{0,1:T(8,128)S(1)}, s32[18,8]{0,1:T(8,128)}, u32[]{:S(2)}) copy-start(s32[18,8]{0,1:T(8,128)} %param.27) | copy-start | bytes 1732
  22.0 6.8 %copy-start.2 = (bf16[8,128,256]{2,1,0:T(8,128)(2,1)S(1)}, bf16[8,128,256]{2,1,0:T(8,128)(2,1)}, u32[]{:S(2)}) copy-start(bf16[8,128,256]{2,1,0:T(8,128)(2,1)} %param.26) | copy-start | bytes 1572868
  22.0 9.5 %copy-start.9 = (s32[2]{0:T(128)S(1)}, s32[2]{0:T(128)}, u32[]{:S(2)}) copy-start(s32[2]{0:T(128)} %param.28) | copy-start | bytes 28
  22.0 23.4 %copy-start.12 = (s32[16]{0:T(128)S(1)}, s32[16]{0:T(128)}, u32[]{:S(2)}) copy-start(s32[16]{0:T(128)} %param.29) | copy-start | bytes 196
  31.5 14.0 %copy-start.10 = (f32[64]{0:T(128)}, f32[64]{0:T(128)S(1)}, u32[]{:S(2)}) copy-start(f32[64]{0:T(128)S(1)} %multiply_power_fusion) | copy-start | bytes 772
  134.5 5.9 %copy-start.11 = (f32[64]{0:T(128)S(1)}, f32[64]{0:T(128)}, u32[]{:S(2)}) copy-start(f32[64]{0:T(128)} %copy-done.10) | copy-start | bytes 772
  134.5 7.9 %copy-start.3 = (bf16[256,8192]{1,0:T(8,128)(2,1)S(1)}, bf16[256,8192]{1,0:T(8,128)(2,1)}, u32[]{:S(2)}) copy-start(bf16[256,8192]{1,0:T(8,128)(2,1)} %copy.47) | copy-start | bytes 12582916
  141.7 7.3 %collective-permute-start.2 = (bf16[512,128]{1,0:T(8,128)(2,1)S(1)}, bf16[512,128]{1,0:T(8,128)(2,1)S(1)}, u32[]{:S(2)}, u32[]{:S(2)}) collective-permute-start(bf16[512,128]{1,0:T(8,128)(2,1)S(1)} %fusion.83), channel_id=1, source_target_pairs={{0,1},{1,0},{2,3},{3,2},{4,5},{5,4},{6,7},{7,6},{8,9},{9,8},{10,11... | collective-permute-start | bytes 393224 | tf_op jit(solution)/shard_map/ppermute | solution.py:16
  148.2 5.2 %copy-start.4 = (bf16[1,8,128,256]{3,2,1,0:T(8,128)(2,1)S(1)}, bf16[1,8,128,256]{3,2,1,0:T(8,128)(2,1)}, u32[]{:S(2)}) copy-start(bf16[1,8,128,256]{3,2,1,0:T(8,128)(2,1)} %bitcast_select_fusion.3) | copy-start | bytes 1572868
  148.9 3.2 collective-permute-start
  149.0 1.1 copy-start.5
  159.3 1.3 copy-start.13
  160.5 135.1 %copy-start.6 = (f32[248,1,4,128]{3,0,2,1:T(8,128)S(1)}, f32[248,1,4,128]{3,0,2,1:T(8,128)}, u32[]{:S(2)}) copy-start(f32[248,1,4,128]{3,0,2,1:T(8,128)} %fusion.54) | copy-start | bytes 1523716
  160.6 137.9 %copy-start.8 = (f32[512]{0:T(512)S(1)}, f32[512]{0:T(512)}, u32[]{:S(2)}) copy-start(f32[512]{0:T(512)} %pad.16.clone) | copy-start | bytes 6148
  295.8 2.7 collective-permute-start.3
  296.6 1.4 collective-permute-start.1
  296.8 1.6 collective-permute-start.4
  309.9 158.4 %copy-start.1 = (bf16[8192,128]{1,0:T(8,128)(2,1)S(1)}, bf16[8192,128]{1,0:T(8,128)(2,1)}, u32[]{:S(2)}) copy-start(bf16[8192,128]{1,0:T(8,128)(2,1)} %param.24) | copy-start | bytes 6291460
Sparse Core Ops, SparseCore 0:
  310.0 156.1 reduce-scatter.1
